TPU v7x, 1024 devices: a whole 4x4x32 slice. The times are simulated.
1024 devices in a mesh: section: 8 (over y_lo, x), half: 2 (over y_hi), dp: 64 (over z, core).
Axes of the slice: x: 4, y: 4 (y_hi: 2, y_lo: 2; y = y_hi * 2 + y_lo), z: 32, core: 2. Of those that a mesh axis runs over, the one named last changes fastest.
Arguments:
- query: bfloat16 [1024, 24576], P('dp', ('section', 'half')), may hold values from -6 to 6
- train: bfloat16 [65536, 24576], P('dp', ('section', 'half')), may hold values from -0.0390625 to 0.0390625
- precond: bfloat16 [96, 256, 256], P(('section', 'half')), may hold values from -0.375 to 0.375
- module_kind: int32 [96], P(('section', 'half')), may hold values from 0 to 6
- kind_scale: float32 [7], replicated, may hold values from 0.25 to 4
Outputs:
- scores: float32 [1024, 65536], P(('section', 'half'), 'dp')
All inputs are finite; a program needn't handle non-finite values.
Results may differ from a plain program's by a relative error of at most 0.0029.
Values may be sent and summed in bfloat16 or wider, within the bound.
A program may use at most 32 MiB of HBM per device.

v0:
```python
import jax
import jax.numpy as jnp
from jax import lax
from jax.sharding import PartitionSpec as P


def per_device(query, train, precond, module_kind, kind_scale):
    q_rows = query.shape[0]
    mods = precond.shape[0]
    feat = precond.shape[1]
    blocks = query.reshape(q_rows, mods, feat)
    pre = jnp.einsum("qmf,mfg->qmg", blocks, precond, preferred_element_type=jnp.float32)
    kinds = jnp.arange(kind_scale.shape[0], dtype=jnp.int32)
    onehot = (module_kind[:, None] == kinds[None, :]).astype(jnp.float32)
    factor = jnp.sum(onehot * kind_scale[None, :], axis=1)
    weighted = (pre * factor[None, :, None]).astype(jnp.bfloat16).reshape(q_rows, mods * feat)
    gathered = lax.dot_general(
        lax.all_gather(weighted, "dp", axis=0, tiled=True),
        train,
        (((1,), (1,)), ((), ())),
        preferred_element_type=jnp.float32,
    )
    return lax.psum_scatter(gathered, ("section", "half"), scatter_dimension=0, tiled=True)


def solution(mesh):
    in_specs = (
        P("dp", ("section", "half")),
        P("dp", ("section", "half")),
        P(("section", "half"), None, None),
        P(("section", "half")),
        P(),
    )
    out_specs = P(("section", "half"), "dp")
    return jax.shard_map(
        per_device, mesh=mesh, in_specs=in_specs, out_specs=out_specs, check_vma=False
    )
```

profile of v0, /device:TPU:34, one launch (start us, length us, event | category | flops | bytes accessed | tf_op | source)
XLA Modules:
  0.0 280.3 jit_solution(18218837792770043187)
XLA Ops:
  6.5 0.0 copy-start
  6.5 0.0 all-gather.2.cloned.1.call-start
  6.5 1.0 select_reduce_fusion
  7.5 1.4 fusion.1
  8.9 0.6 copy.12
  9.6 0.0 all-gather.2.cloned.1.call-update
  9.6 0.0 reduce-scatter.2.cloned.1.call-start
  9.6 145.1 %all-gather.2.cloned.1.call-done = bf16[1024,1536]{1,0:T(8,128)(2,1)} async-done(((bf16[16,1536]{1,0:T(8,128)(2,1)}), bf16[1024,1536]{1,0:T(8,128)(2,1)}) %all-gather.2.cloned.1.call-update) | async-done | bytes 3145744 | tf_op jit(solution)/shard_map/all_gather | solution.py:18
  154.7 0.0 copy-done
  154.7 6.9 %fusion.4 = f32[1024,1024]{1,0:T(8,128)} fusion(bf16[1024,1536]{1,0:T(8,128)(2,1)} %all-gather.2.cloned.1.call-done, bf16[1024,1536]{1,0:T(8,128)(2,1)S(1)} %copy-done), kind=kOutput, calls=%fused_computation.7 | convolution fusion | flops 3221225472 | bytes 10485760 | tf_op jit(solution)/shard_map/dot_general | solution.py:17
  161.6 0.0 reduce-scatter.2.cloned.1.call-update
  161.6 111.8 %reduce-scatter.2.cloned.1.call-done = f32[64,1024]{1,0:T(8,128)} async-done(((f32[1024,1024]{1,0:T(8,128)}), f32[64,1024]{1,0:T(8,128)}) %reduce-scatter.2.cloned.1.call-update) | async-done | bytes 262160 | tf_op jit(solution)/shard_map/reduce_scatter | solution.py:23
Async XLA Ops:
  6.5 148.2 %copy-start = (bf16[1024,1536]{1,0:T(8,128)(2,1)S(1)}, bf16[1024,1536]{1,0:T(8,128)(2,1)}, u32[]{:S(2)}) copy-start(bf16[1024,1536]{1,0:T(8,128)(2,1)} %param.6) | copy-start | bytes 9437188
  6.5 148.1 %all-gather.2.cloned.1.call-start = ((), (), s32[]{:S(2)}) async-start(), calls=%async_computation.1 | async-start | bytes 3194880 | tf_op jit(solution)/shard_map/all_gather | solution.py:18
  9.6 263.9 %reduce-scatter.2.cloned.1.call-start = ((), (), s32[]{:S(2)}) async-start(), calls=%async_computation.2 | async-start | bytes 4456448 | tf_op jit(solution)/shard_map/reduce_scatter | solution.py:23
Sparse Core Ops, SparseCore 0:
  10.1 144.5 all-gather.1
  161.7 111.6 reduce-scatter.1
where the time goes:
time: 280 us
  waiting for transfers between devices  257 us (92%)
  between operations  13.4 us (5%)
  matrix products  8.25 us (3%)
    all_gather x1, waiting for transfers between devices, per_device(): lax.all_gather(weighted, 'dp', axis=0, tiled=True)  145 us
    reduce_scatter x1, waiting for transfers between devices, per_device(): lax.psum_scatter(gathered, ('section', 'half'), scatter_dimension=0, tile...  112 us
    dot_general x1, matrix products, per_device(): lax.dot_general(lax.all_gather(weighted, 'dp', axis=0, tiled=True), train...  6.89 us
  transfers between devices with their start and end apart: 2, of which 2 were waited for; matrix products, arithmetic and copies ran while one was open for 0% of the time, Pallas kernels for 0%

commit v1 on v0

v1 whole, which is shorter than its diff:
```python
import jax
import jax.numpy as jnp
from jax import lax
from jax.experimental import pallas as pl
from jax.experimental.pallas import tpu as pltpu
from jax.sharding import PartitionSpec as P

MESH = pl.DeviceIdType.MESH
PIECES = 3
STRIDE = 3
SIDE = 4


def kernel(
    kind_ref, scale_ref, query_hbm, pre_hbm, train_hbm, out_ref,
    q_v, pre_v, t_v, w_v, s_v, a_v, own_v, g_v, r_v,
    in_sem, ring_send, chain_recv, fill_recv, sib_send, sib_recv, first_send, first_recv, second_send, second_recv,
):
    dp = lax.axis_index("dp")
    sec = lax.axis_index("section")
    half = lax.axis_index("half")
    chips = lax.axis_size("dp") // 2
    halves = lax.axis_size("half")
    owners = lax.axis_size("section") * halves
    share = chips // owners
    me = sec * halves + half
    z = dp // 2
    core = dp % 2
    sign = 1 - 2 * core
    x = sec % SIDE
    y = half * (SIDE // halves) + sec // SIDE
    rows = q_v.shape[0]
    mods, feat, _ = pre_v.shape
    width = w_v.shape[2]
    cols = t_v.shape[0] // SIDE
    both = 2 * rows
    last = chips // 2
    turns = 5 if STRIDE == 3 else 7

    def chip(step):
        return (z + step + 2 * chips) % chips

    def at_xy(px, py):
        low = SIDE // halves
        return {"section": (py % low) * SIDE + px, "half": py // low}

    def along(way, delta):
        return {"dp": chip(sign * delta if way == 0 else -sign * delta) * 2 + core}

    def origin(way, r):
        return chip(-sign * r if way == 0 else sign * r)

    sibling = {"dp": z * 2 + 1 - core}

    load_q = pltpu.make_async_copy(query_hbm, q_v, in_sem.at[0])
    load_pre = pltpu.make_async_copy(pre_hbm, pre_v, in_sem.at[1])
    load_t = pltpu.make_async_copy(train_hbm, t_v, in_sem.at[2])
    load_q.start()
    load_pre.start()
    load_t.start()

    barrier = pltpu.get_barrier_semaphore()
    near = [along(0, 1), along(1, 1), along(0, STRIDE), along(1, STRIDE), sibling]
    for target in near:
        pl.semaphore_signal(barrier, inc=1, device_id=target, device_id_type=MESH)

    def greet(step, carry):
        other = (me + step) % owners
        pl.semaphore_signal(
            barrier, inc=1, device_id={"section": other // halves, "half": other % halves}, device_id_type=MESH)
        return carry

    lax.fori_loop(1, owners, greet, 0)

    load_q.wait()
    load_pre.wait()
    mine = pl.ds(pl.multiple_of(dp * rows, rows), rows)
    for m in range(mods):
        factor = scale_ref[kind_ref[m]]
        pre = jnp.dot(q_v[:, m * feat:(m + 1) * feat], pre_v[m], preferred_element_type=jnp.float32)
        first = m * feat
        w_v[first // width, mine, first % width:first % width + feat] = (pre * factor).astype(jnp.bfloat16)
    pl.semaphore_wait(barrier, owners - 1 + len(near))

    def block(c, lane):
        return pl.ds(pl.multiple_of((c * 2 + lane) * rows, rows), rows)

    def chain(way, r, piece):
        at = w_v.at[piece, block(origin(way, r - STRIDE), core)]
        return pltpu.make_async_remote_copy(
            src_ref=at, dst_ref=at, send_sem=ring_send.at[way], recv_sem=chain_recv.at[way, r, piece],
            device_id=along(way, STRIDE), device_id_type=MESH)

    def chain_wait(way, r, piece):
        at = w_v.at[piece, block(origin(way, r), core)]
        pltpu.make_async_remote_copy(
            src_ref=at, dst_ref=at, send_sem=ring_send.at[way], recv_sem=chain_recv.at[way, r, piece],
            device_id=along(way, STRIDE), device_id_type=MESH).wait_recv()

    def fill(way, r, delta):
        at = w_v.at[:, block(origin(way, r - delta), core)]
        return pltpu.make_async_remote_copy(
            src_ref=at, dst_ref=at, send_sem=ring_send.at[way], recv_sem=fill_recv.at[way, r],
            device_id=along(way, delta), device_id_type=MESH)

    def fill_wait(way, r):
        at = w_v.at[:, block(origin(way, r), core)]
        pltpu.make_async_remote_copy(
            src_ref=at, dst_ref=at, send_sem=ring_send.at[way], recv_sem=fill_recv.at[way, r],
            device_id=along(way, 1), device_id_type=MESH).wait_recv()

    def across(way, r):
        at = w_v.at[:, block(origin(way, r), core)]
        pltpu.make_async_remote_copy(
            src_ref=at, dst_ref=at, send_sem=sib_send, recv_sem=sib_recv.at[way, r],
            device_id=sibling, device_id_type=MESH).start()

    def across_wait(way, r):
        at = w_v.at[:, block(origin(1 - way, r), 1 - core)]
        pltpu.make_async_remote_copy(
            src_ref=at, dst_ref=at, send_sem=sib_send, recv_sem=sib_recv.at[way, r],
            device_id=sibling, device_id_type=MESH).wait_recv()

    def relay(r, ways, on, up, down):
        for piece in range(PIECES):
            for way in ways:
                chain_wait(way, r, piece)
                if way in on:
                    chain(way, r + STRIDE, piece).start()
        for way in ways:
            if way in up:
                fill(way, r + 1, 1).start()
            if way in down:
                fill(way, r - 1, -1).start()
            across(way, r)

    def filled(ways, r):
        for way in ways:
            fill_wait(way, r)
            across(way, r)

    def peer(way, d):
        return at_xy((x + d) % SIDE, y) if way == 0 else at_xy(x, (y + d) % SIDE)

    def first(batch, way, d, n):
        return pltpu.make_async_remote_copy(
            src_ref=s_v.at[batch, way, d - 1, pl.ds(0, n * both)],
            dst_ref=a_v.at[batch, way, d - 1, pl.ds(0, n * both)],
            send_sem=first_send, recv_sem=first_recv.at[batch, way, d - 1],
            device_id=peer(way, d), device_id_type=MESH)

    def multiply(batch, lists):
        for way in range(2):
            for r in lists[way]:
                shared = isinstance(r, int) and r in (0, last)
                across_wait(0 if shared else 1 - way, r)
        for way in range(2):
            chunks = [origin(way, r) for r in lists[way]]
            n = len(chunks)
            lhs = []
            for piece in range(PIECES):
                parts = [w_v[piece, pl.ds(pl.multiple_of(c * both, both), both), :] for c in chunks]
                lhs.append(jnp.concatenate(parts, axis=0) if n > 1 else parts[0])
            for d in (2, 1, 3, 0):
                quarter = ((x if way == 0 else y) + d) % SIDE
                total = None
                for piece in range(PIECES):
                    part = lax.dot_general(
                        lhs[piece],
                        t_v[pl.ds(pl.multiple_of(quarter * cols, cols), cols), piece * width:(piece + 1) * width],
                        (((1,), (1,)), ((), ())), preferred_element_type=jnp.float32)
                    total = part if total is None else total + part
                if d:
                    s_v[batch, way, d - 1, 0:n * both, :] = total.astype(jnp.bfloat16)
                    first(batch, way, d, n).start()
                else:
                    own_v[batch, way, 0:n * both, :] = total

    def reduce(batch, lists):
        for way in range(2):
            n = len(lists[way])
            total = own_v[batch, way, 0:n * both, :]
            for d in (1, 3, 2):
                first(batch, way, d, n).wait_recv()
                total += a_v[batch, way, d - 1, 0:n * both, :].astype(jnp.float32)
            g_v[batch, way, 0:n * both, :] = total.astype(jnp.bfloat16)
            for k, r in enumerate(lists[way]):
                c = origin(way, r)
                owner = c // share
                e = c % share
                quarter, other = (x, y) if way == 0 else (y, x)
                here = pl.ds(k * both, both)

                @pl.when(owner == me)
                def _():
                    r_v[e, quarter, other] = g_v[batch, way, here, :]

                @pl.when(owner != me)
                def _():
                    pltpu.make_async_remote_copy(
                        src_ref=g_v.at[batch, way, here], dst_ref=r_v.at[e, quarter, other],
                        send_sem=second_send, recv_sem=second_recv.at[e, quarter, other],
                        device_id={"section": owner // halves, "half": owner % halves},
                        device_id_type=MESH).start()

    for piece in range(PIECES):
        for way in range(2):
            chain(way, STRIDE, piece).start()
    for way in range(2):
        fill(way, 1, 1).start()
    across(0, 0)

    w01 = (0, 1)
    three = STRIDE == 3

    def batch_of(m):
        rs = [STRIDE * m - 1, STRIDE * m, STRIDE * m + 1] if three else [STRIDE * m, STRIDE * m + 1]
        return [rs, rs]

    head = [[0, 1], [1]]
    tail = [[last - 2, last - 1, last], [last - 2, last - 1]]
    down = w01 if three else ()

    filled(w01, 1)
    relay(STRIDE, w01, w01, w01, down)
    load_t.wait()
    multiply(0, head)

    def turn(j, carry):
        if three:
            filled(w01, STRIDE * (j - 1) - 1)
        filled(w01, STRIDE * (j - 1) + 1)
        relay(STRIDE * j, w01, w01, w01, down)
        multiply(j - 1, batch_of(j - 1))

        @pl.when(j == 2)
        def _():
            reduce(0, head)

        @pl.when(j > 2)
        def _():
            reduce(j - 2, batch_of(j - 2))
        return carry

    lax.fori_loop(2, turns, turn, 0)
    j = turns
    if three:
        filled(w01, STRIDE * (j - 1) - 1)
    filled(w01, STRIDE * (j - 1) + 1)
    if three:
        relay(STRIDE * j, w01, (), (0,), w01)
    else:
        relay(STRIDE * j, w01, (0,), w01, ())
    multiply(j - 1, batch_of(j - 1))
    reduce(j - 2, batch_of(j - 2))
    if three:
        filled(w01, last - 2)
        filled((0,), last)
    else:
        filled(w01, last - 1)
        relay(last, (0,), (), (), ())
    multiply(j, tail)
    reduce(j - 1, batch_of(j - 1))
    reduce(j, tail)

    def collect(i, carry):
        e, quarter, other = i // owners, (i // SIDE) % SIDE, i % SIDE
        c = me * share + e
        step = (c - z + chips) % chips
        ahead = (step * sign + 2 * chips) % chips
        to_x = jnp.where((ahead == 0) | (ahead >= last), 1, 0)
        source_x = to_x * quarter + (1 - to_x) * other
        source_y = to_x * other + (1 - to_x) * quarter

        @pl.when((source_x != x) | (source_y != y))
        def _():
            pltpu.make_async_remote_copy(
                src_ref=r_v.at[e, quarter, other], dst_ref=r_v.at[e, quarter, other],
                send_sem=second_send, recv_sem=second_recv.at[e, quarter, other],
                device_id=sibling, device_id_type=MESH).wait_recv()
        return carry

    lax.fori_loop(0, share * owners, collect, 0)
    for e in range(share):
        for quarter in range(SIDE):
            total = r_v[e, quarter, 0].astype(jnp.float32)
            for other in range(1, SIDE):
                total += r_v[e, quarter, other].astype(jnp.float32)
            out_ref[e * both:(e + 1) * both, quarter * cols:(quarter + 1) * cols] = total

    def sent(ref, sem):
        pltpu.make_async_copy(ref, ref, sem).wait()

    total_rows = chips * both
    sent(w_v.at[:, pl.ds(0, last * rows)], ring_send.at[0])
    sent(w_v.at[:, pl.ds(0, (last - 1) * rows)], ring_send.at[1])
    sent(w_v.at[:, pl.ds(0, chips * rows)], sib_send)
    sent(w_v.at[:, pl.ds(0, total_rows // 2)], first_send)
    sent(w_v.at[0, pl.ds(0, (chips - share) * both // 2)], second_send)


def per_device(query, train, precond, module_kind, kind_scale):
    rows, features = query.shape
    cols = train.shape[0] // SIDE
    devices = lax.axis_size("dp")
    owners = lax.axis_size("section") * lax.axis_size("half")
    total = devices * rows
    share = devices // 2 // owners
    batches = 6 if STRIDE == 3 else 8
    half = devices // 4 + 1
    group = 3 * 2 * rows
    return pl.pallas_call(
        kernel,
        out_shape=jax.ShapeDtypeStruct((total // owners, train.shape[0]), jnp.float32),
        in_specs=[
            pl.BlockSpec(memory_space=pltpu.SMEM),
            pl.BlockSpec(memory_space=pltpu.SMEM),
            pl.BlockSpec(memory_space=pl.ANY),
            pl.BlockSpec(memory_space=pl.ANY),
            pl.BlockSpec(memory_space=pl.ANY),
        ],
        out_specs=pl.BlockSpec(memory_space=pltpu.VMEM),
        scratch_shapes=[
            pltpu.VMEM(query.shape, jnp.bfloat16),
            pltpu.VMEM(precond.shape, jnp.bfloat16),
            pltpu.VMEM(train.shape, jnp.bfloat16),
            pltpu.VMEM((PIECES, total, features // PIECES), jnp.bfloat16),
            pltpu.VMEM((batches, 2, SIDE - 1, group, cols), jnp.bfloat16),
            pltpu.VMEM((batches, 2, SIDE - 1, group, cols), jnp.bfloat16),
            pltpu.VMEM((batches, 2, group, cols), jnp.float32),
            pltpu.VMEM((batches, 2, group, cols), jnp.bfloat16),
            pltpu.VMEM((share, SIDE, SIDE, 2 * rows, cols), jnp.bfloat16),
            pltpu.SemaphoreType.DMA((3,)),
            pltpu.SemaphoreType.DMA((2,)),
            pltpu.SemaphoreType.DMA((2, half, PIECES)),
            pltpu.SemaphoreType.DMA((2, half)),
            pltpu.SemaphoreType.DMA,
            pltpu.SemaphoreType.DMA((2, half)),
            pltpu.SemaphoreType.DMA,
            pltpu.SemaphoreType.DMA((batches, 2, SIDE - 1)),
            pltpu.SemaphoreType.DMA,
            pltpu.SemaphoreType.DMA((share, SIDE, SIDE)),
        ],
        compiler_params=pltpu.CompilerParams(
            collective_id=0, has_side_effects=True, vmem_limit_bytes=48 * 1024 * 1024),
    )(module_kind, kind_scale, query, precond, train)


def solution(mesh):
    in_specs = (
        P("dp", ("section", "half")),
        P("dp", ("section", "half")),
        P(("section", "half"), None, None),
        P(("section", "half")),
        P(),
    )
    out_specs = P(("section", "half"), "dp")
    return jax.shard_map(
        per_device, mesh=mesh, in_specs=in_specs, out_specs=out_specs, check_vma=False
    )
```

time: 280 us -> 84.6 us (0.30)
  the two profiles are of different devices: /device:TPU:34 before, /device:TPU:40 now
where the time goes in v1:
time: 84.6 us; the launch traced here: 84.3 us
  Pallas kernels  78.4 us (93%)
  local copies, waits for them, and re-layouts  5.83 us (7%)
    pallas_call x1, Pallas kernels, per_device(): pl.pallas_call(kernel, out_shape=jax.ShapeDtypeStruct((total // owners, t...  78.4 us
    unnamed x11, local copies, waits for them, and re-layouts  5.83 us

profile of v1, /device:TPU:40, one launch (start us, length us, event | category | flops | bytes accessed | tf_op | source)
XLA Modules:
  0.0 84.3 jit_solution(8092310473836040747)
XLA Ops:
  0.0 0.0 copy-start
  0.0 1.9 %copy-done = bf16[1024,1536]{1,0:T(8,128)(2,1)S(1)} copy-done((bf16[1024,1536]{1,0:T(8,128)(2,1)S(1)}, bf16[1024,1536]{1,0:T(8,128)(2,1)}, u32[]{:S(2)}) %copy-start) | copy-done | bytes 3145752
  1.9 0.0 copy-start.1
  1.9 1.1 %copy-done.1 = bf16[6,256,256]{2,1,0:T(8,128)(2,1)S(1)} copy-done((bf16[6,256,256]{2,1,0:T(8,128)(2,1)S(1)}, bf16[6,256,256]{2,1,0:T(8,128)(2,1)}, u32[]{:S(2)}) %copy-start.1) | copy-done | bytes 786456
  3.0 0.0 copy-start.2
  3.0 0.8 copy-done.2
  3.8 0.0 copy-start.3
  3.8 0.7 copy-done.3
  4.5 0.0 copy-start.4
  4.5 0.7 copy-done.4
  5.1 78.4 %shard_map.55 = f32[64,1024]{1,0:T(8,128)S(1)} custom-call(s32[6]{0:T(128)S(1)} %copy-done.3, f32[7]{0:T(128)S(1)} %copy-done.4, bf16[16,1536]{1,0:T(8,128)(2,1)S(1)} %copy-done.2, bf16[6,256,256]{2,1,0:T(8,128)(2,1)S(1)} %copy-done.1, bf16[1024,1536]{1,0:T(8,128)(2,1)S(1)} %copy-done), custom_call_target="tpu_custom_call" | custom-call | tf_op jit(solution)/shard_map/pallas_call | solution.py:312
  83.6 0.7 copy.7
Async XLA Ops:
  0.0 1.9 %copy-start = (bf16[1024,1536]{1,0:T(8,128)(2,1)S(1)}, bf16[1024,1536]{1,0:T(8,128)(2,1)}, u32[]{:S(2)}) copy-start(bf16[1024,1536]{1,0:T(8,128)(2,1)} %train_hbm.1) | copy-start | bytes 9437188
  1.9 1.1 %copy-start.1 = (bf16[6,256,256]{2,1,0:T(8,128)(2,1)S(1)}, bf16[6,256,256]{2,1,0:T(8,128)(2,1)}, u32[]{:S(2)}) copy-start(bf16[6,256,256]{2,1,0:T(8,128)(2,1)} %pre_hbm.1) | copy-start | bytes 2359300
  3.0 0.8 copy-start.2
  3.8 0.7 copy-start.3
  4.5 0.7 copy-start.4

commit v2 on v1

--- a/solution.py
+++ b/solution.py
@@ -8,12 +8,13 @@
 MESH = pl.DeviceIdType.MESH
 PIECES = 3
 STRIDE = 3
+TURNS = 5
 SIDE = 4
 
 
 def kernel(
-    kind_ref, scale_ref, query_hbm, pre_hbm, train_hbm, out_ref,
-    q_v, pre_v, t_v, w_v, s_v, a_v, own_v, g_v, r_v,
+    kind_hbm, scale_hbm, query_hbm, pre_hbm, train_hbm, r_hbm,
+    kind_ref, scale_ref, q_v, pre_v, t_v, w_v, s_v, a_v, own_v, g_v,
     in_sem, ring_send, chain_recv, fill_recv, sib_send, sib_recv, first_send, first_recv, second_send, second_recv,
 ):
     dp = lax.axis_index("dp")
@@ -35,7 +36,6 @@
     cols = t_v.shape[0] // SIDE
     both = 2 * rows
     last = chips // 2
-    turns = 5 if STRIDE == 3 else 7
 
     def chip(step):
         return (z + step + 2 * chips) % chips
@@ -47,6 +47,9 @@
     def along(way, delta):
         return {"dp": chip(sign * delta if way == 0 else -sign * delta) * 2 + core}
 
+    def beyond(way, delta):
+        return {"dp": chip(sign * delta if way == 0 else -sign * delta) * 2 + 1 - core}
+
     def origin(way, r):
         return chip(-sign * r if way == 0 else sign * r)
 
@@ -55,12 +58,16 @@
     load_q = pltpu.make_async_copy(query_hbm, q_v, in_sem.at[0])
     load_pre = pltpu.make_async_copy(pre_hbm, pre_v, in_sem.at[1])
     load_t = pltpu.make_async_copy(train_hbm, t_v, in_sem.at[2])
+    load_kind = pltpu.make_async_copy(kind_hbm, kind_ref, in_sem.at[3])
+    load_scale = pltpu.make_async_copy(scale_hbm, scale_ref, in_sem.at[4])
     load_q.start()
+    load_kind.start()
+    load_scale.start()
     load_pre.start()
     load_t.start()
 
     barrier = pltpu.get_barrier_semaphore()
-    near = [along(0, 1), along(1, 1), along(0, STRIDE), along(1, STRIDE), sibling]
+    near = [along(0, 1), along(1, 1), along(0, STRIDE), along(1, STRIDE), sibling, beyond(0, 1), beyond(1, 1)]
     for target in near:
         pl.semaphore_signal(barrier, inc=1, device_id=target, device_id_type=MESH)
 
@@ -73,6 +80,8 @@
     lax.fori_loop(1, owners, greet, 0)
 
     load_q.wait()
+    load_kind.wait()
+    load_scale.wait()
     load_pre.wait()
     mine = pl.ds(pl.multiple_of(dp * rows, rows), rows)
     for m in range(mods):
@@ -114,6 +123,12 @@
         pltpu.make_async_remote_copy(
             src_ref=at, dst_ref=at, send_sem=sib_send, recv_sem=sib_recv.at[way, r],
             device_id=sibling, device_id_type=MESH).start()
+
+    def cross(way, r, delta):
+        at = w_v.at[:, block(origin(way, r - delta), core)]
+        pltpu.make_async_remote_copy(
+            src_ref=at, dst_ref=at, send_sem=sib_send, recv_sem=sib_recv.at[way, r],
+            device_id=beyond(way, delta), device_id_type=MESH).start()
 
     def across_wait(way, r):
         at = w_v.at[:, block(origin(1 - way, r), 1 - core)]
@@ -191,14 +206,18 @@
                 quarter, other = (x, y) if way == 0 else (y, x)
                 here = pl.ds(k * both, both)
 
+                slot = r_hbm.at[
+                    other, pl.ds(pl.multiple_of(e * both, both), both),
+                    pl.ds(pl.multiple_of(quarter * cols, cols), cols)]
+
                 @pl.when(owner == me)
                 def _():
-                    r_v[e, quarter, other] = g_v[batch, way, here, :]
+                    pltpu.make_async_copy(g_v.at[batch, way, here], slot, in_sem.at[5]).start()
 
                 @pl.when(owner != me)
                 def _():
                     pltpu.make_async_remote_copy(
-                        src_ref=g_v.at[batch, way, here], dst_ref=r_v.at[e, quarter, other],
+                        src_ref=g_v.at[batch, way, here], dst_ref=slot,
                         send_sem=second_send, recv_sem=second_recv.at[e, quarter, other],
                         device_id={"section": owner // halves, "half": owner % halves},
                         device_id_type=MESH).start()
@@ -211,56 +230,53 @@
     across(0, 0)
 
     w01 = (0, 1)
-    three = STRIDE == 3
-
-    def batch_of(m):
-        rs = [STRIDE * m - 1, STRIDE * m, STRIDE * m + 1] if three else [STRIDE * m, STRIDE * m + 1]
+
+    def batch_of(j):
+        rs = [STRIDE * j - 4, STRIDE * j - 2, STRIDE * j]
         return [rs, rs]
 
-    head = [[0, 1], [1]]
-    tail = [[last - 2, last - 1, last], [last - 2, last - 1]]
-    down = w01 if three else ()
-
+    head = [[0, 1, STRIDE], [1, STRIDE]]
+    tail = [[last - 2, last], [last - 2]]
+
+    relay(STRIDE, w01, w01, w01, w01)
     filled(w01, 1)
-    relay(STRIDE, w01, w01, w01, down)
+    relay(STRIDE * 2, w01, w01, w01, w01)
     load_t.wait()
     multiply(0, head)
+    filled(w01, STRIDE * 2 - 4)
+    filled(w01, STRIDE * 2 - 2)
 
     def turn(j, carry):
-        if three:
-            filled(w01, STRIDE * (j - 1) - 1)
-        filled(w01, STRIDE * (j - 1) + 1)
-        relay(STRIDE * j, w01, w01, w01, down)
-        multiply(j - 1, batch_of(j - 1))
-
-        @pl.when(j == 2)
+        relay(STRIDE * j, w01, w01, w01, w01)
+        multiply(j - 2, batch_of(j - 1))
+
+        @pl.when(j == 3)
         def _():
             reduce(0, head)
 
-        @pl.when(j > 2)
+        @pl.when(j > 3)
         def _():
-            reduce(j - 2, batch_of(j - 2))
+            reduce(j - 3, batch_of(j - 2))
+        filled(w01, STRIDE * j - 4)
+        filled(w01, STRIDE * j - 2)
         return carry
 
-    lax.fori_loop(2, turns, turn, 0)
-    j = turns
-    if three:
-        filled(w01, STRIDE * (j - 1) - 1)
-    filled(w01, STRIDE * (j - 1) + 1)
-    if three:
-        relay(STRIDE * j, w01, (), (0,), w01)
-    else:
-        relay(STRIDE * j, w01, (0,), w01, ())
-    multiply(j - 1, batch_of(j - 1))
-    reduce(j - 2, batch_of(j - 2))
-    if three:
-        filled(w01, last - 2)
-        filled((0,), last)
-    else:
-        filled(w01, last - 1)
-        relay(last, (0,), (), (), ())
+    lax.fori_loop(3, TURNS, turn, 0)
+    j = TURNS
+    relay(STRIDE * j, w01, (), (0,), w01)
+    cross(0, last, 1)
+    cross(0, last - 2, -1)
+    cross(1, last - 2, -1)
+    filled(w01, STRIDE * j - 4)
+    filled(w01, STRIDE * j - 2)
+    multiply(j - 2, batch_of(j - 1))
+    reduce(j - 3, batch_of(j - 2))
+    multiply(j - 1, batch_of(j))
+    reduce(j - 2, batch_of(j - 1))
+    for way, r in ((0, last), (0, last - 2), (1, last - 2)):
+        fill_wait(way, r)
     multiply(j, tail)
-    reduce(j - 1, batch_of(j - 1))
+    reduce(j - 1, batch_of(j))
     reduce(j, tail)
 
     def collect(i, carry):
@@ -274,29 +290,26 @@
 
         @pl.when((source_x != x) | (source_y != y))
         def _():
+            slot = r_hbm.at[
+                other, pl.ds(pl.multiple_of(e * both, both), both),
+                pl.ds(pl.multiple_of(quarter * cols, cols), cols)]
             pltpu.make_async_remote_copy(
-                src_ref=r_v.at[e, quarter, other], dst_ref=r_v.at[e, quarter, other],
+                src_ref=slot, dst_ref=slot,
                 send_sem=second_send, recv_sem=second_recv.at[e, quarter, other],
                 device_id=sibling, device_id_type=MESH).wait_recv()
         return carry
 
     lax.fori_loop(0, share * owners, collect, 0)
-    for e in range(share):
-        for quarter in range(SIDE):
-            total = r_v[e, quarter, 0].astype(jnp.float32)
-            for other in range(1, SIDE):
-                total += r_v[e, quarter, other].astype(jnp.float32)
-            out_ref[e * both:(e + 1) * both, quarter * cols:(quarter + 1) * cols] = total
-
     def sent(ref, sem):
         pltpu.make_async_copy(ref, ref, sem).wait()
 
     total_rows = chips * both
+    sent(g_v.at[0, 0, pl.ds(0, share * both)], in_sem.at[5])
     sent(w_v.at[:, pl.ds(0, last * rows)], ring_send.at[0])
     sent(w_v.at[:, pl.ds(0, (last - 1) * rows)], ring_send.at[1])
     sent(w_v.at[:, pl.ds(0, chips * rows)], sib_send)
     sent(w_v.at[:, pl.ds(0, total_rows // 2)], first_send)
-    sent(w_v.at[0, pl.ds(0, (chips - share) * both // 2)], second_send)
+    sent(w_v.at[0, pl.ds(0, (chips - share) * both * cols // width)], second_send)
 
 
 def per_device(query, train, precond, module_kind, kind_scale):
@@ -306,21 +319,23 @@
     owners = lax.axis_size("section") * lax.axis_size("half")
     total = devices * rows
     share = devices // 2 // owners
-    batches = 6 if STRIDE == 3 else 8
+    batches = TURNS + 1
     half = devices // 4 + 1
     group = 3 * 2 * rows
-    return pl.pallas_call(
+    parts = pl.pallas_call(
         kernel,
-        out_shape=jax.ShapeDtypeStruct((total // owners, train.shape[0]), jnp.float32),
+        out_shape=jax.ShapeDtypeStruct((SIDE, total // owners, train.shape[0]), jnp.bfloat16),
         in_specs=[
-            pl.BlockSpec(memory_space=pltpu.SMEM),
-            pl.BlockSpec(memory_space=pltpu.SMEM),
-            pl.BlockSpec(memory_space=pl.ANY),
-            pl.BlockSpec(memory_space=pl.ANY),
-            pl.BlockSpec(memory_space=pl.ANY),
+            pl.BlockSpec(memory_space=pltpu.HBM),
+            pl.BlockSpec(memory_space=pltpu.HBM),
+            pl.BlockSpec(memory_space=pltpu.HBM),
+            pl.BlockSpec(memory_space=pltpu.HBM),
+            pl.BlockSpec(memory_space=pltpu.HBM),
         ],
-        out_specs=pl.BlockSpec(memory_space=pltpu.VMEM),
+        out_specs=pl.BlockSpec(memory_space=pltpu.HBM),
         scratch_shapes=[
+            pltpu.SMEM(module_kind.shape, jnp.int32),
+            pltpu.SMEM(kind_scale.shape, jnp.float32),
             pltpu.VMEM(query.shape, jnp.bfloat16),
             pltpu.VMEM(precond.shape, jnp.bfloat16),
             pltpu.VMEM(train.shape, jnp.bfloat16),
@@ -329,8 +344,7 @@
             pltpu.VMEM((batches, 2, SIDE - 1, group, cols), jnp.bfloat16),
             pltpu.VMEM((batches, 2, group, cols), jnp.float32),
             pltpu.VMEM((batches, 2, group, cols), jnp.bfloat16),
-            pltpu.VMEM((share, SIDE, SIDE, 2 * rows, cols), jnp.bfloat16),
-            pltpu.SemaphoreType.DMA((3,)),
+            pltpu.SemaphoreType.DMA((6,)),
             pltpu.SemaphoreType.DMA((2,)),
             pltpu.SemaphoreType.DMA((2, half, PIECES)),
             pltpu.SemaphoreType.DMA((2, half)),
@@ -342,8 +356,9 @@
             pltpu.SemaphoreType.DMA((share, SIDE, SIDE)),
         ],
         compiler_params=pltpu.CompilerParams(
-            collective_id=0, has_side_effects=True, vmem_limit_bytes=48 * 1024 * 1024),
+            collective_id=0, has_side_effects=True, vmem_limit_bytes=67043328),
     )(module_kind, kind_scale, query, precond, train)
+    return jnp.sum(parts.astype(jnp.float32), axis=0)
 
 
 def solution(mesh):

time: 84.6 us -> 76.1 us (0.90)
  the two profiles are of different devices: /device:TPU:40 before, /device:TPU:54 now
where the time goes in v2:
time: 76.1 us; the launch traced here: 75.9 us
  Pallas kernels  74.1 us (97%)
  other arithmetic  1.84 us (2%)
    pallas_call x1, Pallas kernels, per_device(): pl.pallas_call(kernel, out_shape=jax.ShapeDtypeStruct((SIDE, total // own...  74.1 us
    reduce_sum x1, other arithmetic, per_device(): return jnp.sum(parts.astype(jnp.float32), axis=0)  1.84 us

profile of v2, /device:TPU:54, one launch (start us, length us, event | category | flops | bytes accessed | tf_op | source)
XLA Modules:
  0.0 75.9 jit_solution(7196968829693004358)
XLA Ops:
  0.0 74.1 %shard_map.55 = bf16[4,64,1024]{2,1,0:T(8,128)(2,1)} custom-call(s32[6]{0:T(128)} %kind_hbm.1, f32[7]{0:T(128)} %scale_hbm.1, bf16[16,1536]{1,0:T(8,128)(2,1)} %query_hbm.1, bf16[6,256,256]{2,1,0:T(8,128)(2,1)} %pre_hbm.1, bf16[1024,1536]{1,0:T(8,128)(2,1)} %train_hbm.1), custom_call_target="tpu_custom_call" | custom-call | tf_op jit(solution)/shard_map/pallas_call | solution.py:325
  74.1 1.8 %convert_reduce_fusion = f32[64,1024]{1,0:T(8,128)} fusion(bf16[4,64,1024]{2,1,0:T(8,128)(2,1)} %shard_map.55), kind=kLoop, calls=%fused_computation | loop fusion | flops 458752 | bytes 786432 | tf_op jit(solution)/shard_map/reduce_sum | solution.py:361
